TPU v7x, 128 devices: a whole 4x4x4 slice. The times are simulated.
128 devices in a mesh: src: 16 (over x, z_lo, core), freq: 8 (over y, z_hi).
Axes of the slice: x: 4, y: 4, z: 4 (z_hi: 2, z_lo: 2; z = z_hi * 2 + z_lo), core: 2. Of those that a mesh axis runs over, the one named last changes fastest.
Arguments:
- receivers: bfloat16 [8, 16, 2, 256, 512], P('freq', 'src'), may hold values from -6 to 6
- data: bfloat16 [8, 2, 8192, 2048], P('freq', None, None, 'src'), may hold values from -0.046875 to 0.046875
- block_of_slot: int32 [16], replicated, may hold values from 0 to 15, each once
- receiver_order: int32 [256], replicated, may hold values from 0 to 255, each once
Outputs:
- traces: bfloat16 [256, 2048, 256], P('freq', 'src')
Inputs may be any that keep to these rules, and one draw needn't show every extreme that they name: `block_of_slot`: each of the 16 bounce blocks is held in exactly one slot. `receiver_order`: each receiver appears in exactly one trace row.
All inputs are finite; a program needn't handle non-finite values.
Results may differ from a plain program's by a relative error of at most 0.0049.
Values may be sent and summed in bfloat16 or wider, within the bound.
A program may use at most 64 MiB of HBM per device.

v0:
```python
import math
import jax
import jax.numpy as jnp
import numpy as np
from jax import lax
from jax.sharding import PartitionSpec as P

NT = 256


def tables(count):
    times = np.arange(NT)
    bins = (2 * np.arange(count) + 1) * (NT // (4 * count))
    angle = bins[:, None] * times[None, :] % NT * (2.0 * math.pi / NT)
    full = np.stack([np.cos(angle), -np.sin(angle)], 1) * count ** (-0.5)
    return full.astype(np.float32)


def body(receivers, data, block_of_slot, receiver_order):
    width = receivers.shape[4]
    blocks = lax.all_gather(receivers[0], "src", axis=0, tiled=True)
    slots = blocks.shape[0]
    rows = data[0].reshape(2, slots, width, data.shape[3])
    slot_of_block = jnp.argsort(block_of_slot)
    moved = jnp.take(blocks, slot_of_block, axis=0)
    acc = jnp.einsum("jcrk,djks->cdrs", moved, rows, preferred_element_type=jnp.float32)
    spectra = jnp.stack([acc[0, 0] - acc[1, 1], acc[0, 1] + acc[1, 0]], 0).astype(jnp.bfloat16)
    ordered = jnp.take(spectra, receiver_order, axis=1)[None]
    got = lax.all_to_all(ordered, "freq", split_axis=2, concat_axis=0, tiled=True)
    table = jnp.asarray(tables(got.shape[0]))
    high = table.astype(jnp.bfloat16)
    low = (table - high.astype(jnp.float32)).astype(jnp.bfloat16)
    value = jnp.einsum("fcrs,fct->rst", got, high, preferred_element_type=jnp.float32)
    value = value + jnp.einsum("fcrs,fct->rst", got, low, preferred_element_type=jnp.float32)
    return value.astype(jnp.bfloat16)


def solution(mesh):
    placed = (P("freq", "src", None, None, None), P("freq", None, None, "src"), P(), P())
    return jax.shard_map(
        body, mesh=mesh, in_specs=placed, out_specs=P("freq", "src", None), check_vma=False
    )
```

profile of v0, /device:TPU:0, one launch (start us, length us, event | category | flops | bytes accessed | tf_op | source)
XLA Modules:
  0.0 104.4 jit_solution(16391787386407409647)
XLA Ops:
  6.5 0.0 all-gather.3.cloned.1.call-start
  6.5 0.7 all-gather.3.cloned.1.call-update
  7.3 1.9 %sort.17 = (s32[16]{0:T(128)}, s32[16]{0:T(128)S(1)}) sort(s32[16]{0:T(128)} %param.7, s32[16]{0:T(128)S(1)} %iota.4), dimensions={0}, to_apply=%region_0.0 | sort | flops 64 | bytes 256 | tf_op jit(solution)/shard_map/jit(argsort)/sort | solution.py:24
  9.2 0.7 compare_select_fusion
  9.9 0.7 compare_and_fusion.1
  10.6 53.1 %all-gather.3.cloned.1.call-done = bf16[16,1,2,256,512]{4,3,2,1,0:T(8,128)(2,1)} async-done(((bf16[1,1,2,256,512]{4,3,2,1,0:T(8,128)(2,1)}), bf16[16,1,2,256,512]{4,3,2,1,0:T(8,128)(2,1)}) %all-gather.3.cloned.1.call-update) | async-done | bytes 8388624 | tf_op jit(solution)/shard_map/all_gather | solution.py:21
  63.7 8.1 %gather_fusion = bf16[16,2,256,512]{3,2,1,0:T(8,128)(2,1)} fusion(bf16[16,2,256,512]{3,2,1,0:T(8,128)(2,1)} %bitcast.46, s32[1024]{0:T(1024)S(1)} %pad_clamp_fusion.1), kind=kCustom, calls=%fused_computation | custom fusion | bytes 16777280 | tf_op jit(solution)/shard_map/jit(_take)/gather | solution.py:25
  71.8 0.0 copy-start
  71.8 0.0 copy-start.1
  71.8 7.0 %fusion.3 = f32[2,2,256,128]{3,2,1,0:T(8,128)S(1)} fusion(bf16[2,16,512,128,1]{3,2,1,0,4:T(8,128)(2,1)} %bitcast.49, bf16[16,2,256,512]{3,2,1,0:T(8,128)(2,1)} %gather_fusion, pred[16]{0:T(512)(128)(4,1)S(1)} %compare_and_fusion), kind=kOutput, calls=%fused_computation.7 | convolution fusion | flops 2151677952 | bytes 13107216 | tf_op jit(solution)/shard_map/jcrk,djks->cdrs/dot_general | solution.py:26
  78.8 0.1 copy.15
  79.0 0.9 gather_fusion.1
  79.9 0.3 fusion.11
  80.3 14.4 %all_to_all.18 = bf16[1,2,256,128]{3,1,0,2:T(2,128)(2,1)S(1)} all-to-all(bf16[1,2,256,128]{3,1,0,2:T(2,128)(2,1)S(1)} %fusion.11), channel_id=1, replica_groups=mesh['src'=16,'freq'=8] {'freq'}, dimensions={2} | all-to-all | bytes 262144 | tf_op jit(solution)/shard_map/all_to_all | solution.py:29
  94.7 0.0 copy-done
  94.7 0.8 fusion.9
  95.5 0.0 copy-done.1
  95.5 2.1 %fusion.2 = bf16[32,128,256]{2,1,0:T(8,128)(2,1)} fusion(f32[32,128,256,1]{2,1,3,0:T(8,128)S(1)} %fusion.9, bf16[8,2,256,1]{2,0,1,3:T(8,128)(2,1)S(1)} %copy-done.1, bf16[1,2,8,32,128]{4,1,3,2,0:T(2,128)(2,1)S(1)} %bitcast.48), kind=kOutput, calls=%fused_computation.6 | convolution fusion | flops 35651584 | bytes 6430720 | tf_op jit(solution)/shard_map/fcrs,fct->rst/dot_general | solution.py:34
  (7 shorter events, 0.1 us)
Async XLA Ops:
  6.5 57.1 %all-gather.3.cloned.1.call-start = ((), (), s32[]{:S(2)}) async-start(), calls=%async_computation.1 | async-start | bytes 8912896 | tf_op jit(solution)/shard_map/all_gather | solution.py:21
  71.8 22.9 %copy-start = (bf16[8,2,256,1]{2,0,1,3:T(8,128)(2,1)S(1)}, bf16[8,2,256,1]{2,0,1,3:T(8,128)(2,1)}, u32[]{:S(2)}) copy-start(bf16[8,2,256,1]{2,0,1,3:T(8,128)(2,1)} %constant.39) | copy-start | bytes 24580
  71.8 23.7 %copy-start.1 = (bf16[8,2,256,1]{2,0,1,3:T(8,128)(2,1)S(1)}, bf16[8,2,256,1]{2,0,1,3:T(8,128)(2,1)}, u32[]{:S(2)}) copy-start(bf16[8,2,256,1]{2,0,1,3:T(8,128)(2,1)} %constant.40) | copy-start | bytes 24580
Sparse Core Ops, SparseCore 0:
  9.0 54.5 all-gather.2
where the time goes:
time: 105 us; the launch traced here: 104 us
  waiting for transfers between devices  53.8 us (51%)
  blocking collectives  14.4 us (14%)
  between operations  13.5 us (13%)
  matrix products  9.82 us (9%)
  local copies, waits for them, and re-layouts  9.21 us (9%)
  other arithmetic  3.68 us (4%)
    all_gather x1, waiting for transfers between devices, body(): blocks = lax.all_gather(receivers[0], 'src', axis=0, tiled=True)  53.1 us
    all_to_all x1, blocking collectives, body(): lax.all_to_all(ordered, 'freq', split_axis=2, concat_axis=0, tiled=True)  14.4 us
    gather x1, local copies, waits for them, and re-layouts, body(): moved = jnp.take(blocks, slot_of_block, axis=0)  8.13 us
    dot_general x1, matrix products, body(): jnp.einsum('jcrk,djks->cdrs', moved, rows, preferred_element_type=jnp.flo...  6.97 us
  transfers between devices with their start and end apart: 1, of which 1 were waited for; matrix products, arithmetic and copies ran while one was open for 3% of the time, Pallas kernels for 0%

commit v1 on v0

--- a/solution.py
+++ b/solution.py
@@ -18,7 +18,9 @@
 
 def body(receivers, data, block_of_slot, receiver_order):
     width = receivers.shape[4]
-    blocks = lax.all_gather(receivers[0], "src", axis=0, tiled=True)
+    blocks = jnp.concatenate(
+        lax.all_to_all(jnp.stack([receivers[0]] * lax.axis_size("src")), "src", 0, 0), axis=0
+    )
     slots = blocks.shape[0]
     rows = data[0].reshape(2, slots, width, data.shape[3])
     slot_of_block = jnp.argsort(block_of_slot)

time: 105 us -> 178 us (1.70)
  waiting for transfers between devices: 53.8 us -> 131 us
  between operations: 13.5 us -> 0.12 us
  starting transfers between devices: 0.01 us -> 6.05 us
  local copies, waits for them, and re-layouts: 9.21 us -> 14.4 us
  other arithmetic: 3.68 us -> 1.67 us
    all_to_all x0 -> x1, waiting for transfers between devices: none -> 131 us  [body(): lax.all_to_all(jnp.stack([receivers[0]] * lax.axis_size('src')), 'src', 0...]
    all_gather x1 -> x0, waiting for transfers between devices: 53.1 us -> none  [body(): blocks = lax.all_gather(receivers[0], 'src', axis=0, tiled=True)]
    all_to_all x0 -> x1, starting transfers between devices: none -> 6.05 us  [body(): lax.all_to_all(jnp.stack([receivers[0]] * lax.axis_size('src')), 'src', 0...]
    another operation x0 -> x1, local copies, waits for them, and re-layouts: none -> 5.2 us  [body(): jnp.stack([receivers[0]] * lax.axis_size('src'))]
  transfers between devices with their start and end apart: 1 -> 1, of which waited for: 1 -> 1; matrix products, arithmetic and copies ran while one was open for 3% -> 1% of each run, Pallas kernels for 0% -> 0%
where the time goes in v1:
time: 178 us
  waiting for transfers between devices  131 us (74%)
  blocking collectives  15.2 us (9%)
  local copies, waits for them, and re-layouts  14.4 us (8%)
  matrix products  9.82 us (6%)
  starting transfers between devices  6.05 us (3%)
    all_to_all x1, waiting for transfers between devices, body(): lax.all_to_all(jnp.stack([receivers[0]] * lax.axis_size('src')), 'src', 0...  131 us
    all_to_all x1, blocking collectives, body(): lax.all_to_all(ordered, 'freq', split_axis=2, concat_axis=0, tiled=True)  15.2 us
    gather x1, local copies, waits for them, and re-layouts, body(): moved = jnp.take(blocks, slot_of_block, axis=0)  8.13 us
    dot_general x1, matrix products, body(): jnp.einsum('jcrk,djks->cdrs', moved, rows, preferred_element_type=jnp.flo...  6.97 us
    all_to_all x1, starting transfers between devices, body(): lax.all_to_all(jnp.stack([receivers[0]] * lax.axis_size('src')), 'src', 0...  6.05 us
    another operation x1, local copies, waits for them, and re-layouts, body(): jnp.stack([receivers[0]] * lax.axis_size('src'))  5.2 us
  transfers between devices with their start and end apart: 1, of which 1 were waited for; matrix products, arithmetic and copies ran while one was open for 1% of the time, Pallas kernels for 0%

profile of v1, /device:TPU:0, one launch (start us, length us, event | category | flops | bytes accessed | tf_op | source)
XLA Modules:
  0.0 177.9 jit_solution(1676271520003362899)
XLA Ops:
  0.0 5.2 %stack.9 = bf16[16,1,2,256,512]{4,3,2,1,0:T(8,128)(2,1)} broadcast(bf16[2,256,512]{2,1,0:T(8,128)(2,1)} %bitcast.49), dimensions={2,3,4} | broadcast | bytes 8912896 | tf_op jit(solution)/shard_map/stack | solution.py:22
  5.2 0.0 copy-start.3
  5.2 0.0 copy-start.2
  5.2 6.1 %all-to-all-start = ((bf16[16,1,2,256,512]{4,3,2,1,0:T(8,128)(2,1)}), bf16[16,1,2,256,512]{4,3,2,1,0:T(8,128)(2,1)}, u32[]{:S(2)}, u32[]{:S(2)}) async-start(bf16[16,1,2,256,512]{4,3,2,1,0:T(8,128)(2,1)} %stack.9), calls=%async_computation | async-start | bytes 16777216 | tf_op jit(solution)/shard_map/all_to_all | solution.py:22
  11.3 0.0 copy-done.3
  11.3 1.2 sort.17
  12.5 0.0 copy-done.2
  12.6 130.6 %all-to-all-done = bf16[16,1,2,256,512]{4,3,2,1,0:T(8,128)(2,1)} async-done(((bf16[16,1,2,256,512]{4,3,2,1,0:T(8,128)(2,1)}), bf16[16,1,2,256,512]{4,3,2,1,0:T(8,128)(2,1)}, u32[]{:S(2)}, u32[]{:S(2)}) %all-to-all-start) | async-done | bytes 8388640 | tf_op jit(solution)/shard_map/all_to_all | solution.py:22
  143.2 8.1 %gather_fusion = bf16[16,2,256,512]{3,2,1,0:T(8,128)(2,1)} fusion(bf16[16,2,256,512]{3,2,1,0:T(8,128)(2,1)} %bitcast.1, s32[1024]{0:T(1024)S(1)} %pad_clamp_fusion.1), kind=kCustom, calls=%fused_computation | custom fusion | bytes 16777280 | tf_op jit(solution)/shard_map/jit(_take)/gather | solution.py:27
  151.4 0.0 copy-start
  151.4 0.0 copy-start.1
  151.4 7.0 %fusion.3 = f32[2,2,256,128]{3,2,1,0:T(8,128)S(1)} fusion(bf16[2,16,512,128,1]{3,2,1,0,4:T(8,128)(2,1)} %bitcast.50, bf16[16,2,256,512]{3,2,1,0:T(8,128)(2,1)} %gather_fusion, pred[16]{0:T(512)(128)(4,1)S(1)} %compare_and_fusion), kind=kOutput, calls=%fused_computation.7 | convolution fusion | flops 2151677952 | bytes 13107216 | tf_op jit(solution)/shard_map/jcrk,djks->cdrs/dot_general | solution.py:28
  158.4 0.1 copy.14
  158.6 0.9 gather_fusion.1
  159.5 0.3 fusion.11
  159.8 15.2 %all_to_all.23 = bf16[1,2,256,128]{3,1,0,2:T(2,128)(2,1)S(1)} all-to-all(bf16[1,2,256,128]{3,1,0,2:T(2,128)(2,1)S(1)} %fusion.11), channel_id=1, replica_groups=mesh['src'=16,'freq'=8] {'freq'}, dimensions={2} | all-to-all | bytes 262144 | tf_op jit(solution)/shard_map/all_to_all | solution.py:31
  175.0 0.0 copy-done
  175.0 0.8 fusion.9
  175.8 0.0 copy-done.1
  175.8 2.1 %fusion.2 = bf16[32,128,256]{2,1,0:T(8,128)(2,1)} fusion(f32[32,128,256,1]{2,1,3,0:T(8,128)S(1)} %fusion.9, bf16[8,2,256,1]{2,0,1,3:T(8,128)(2,1)S(1)} %copy-done.1, bf16[1,2,8,32,128]{4,1,3,2,0:T(2,128)(2,1)S(1)} %bitcast.48), kind=kOutput, calls=%fused_computation.6 | convolution fusion | flops 35651584 | bytes 6430720 | tf_op jit(solution)/shard_map/fcrs,fct->rst/dot_general | solution.py:36
  (9 shorter events, 0.1 us)
Async XLA Ops:
  5.2 6.1 %copy-start.3 = (s32[16]{0:T(128)S(1)}, s32[16]{0:T(128)}, u32[]{:S(2)}) copy-start(s32[16]{0:T(128)} %param.7) | copy-start | bytes 196
  5.2 7.3 %copy-start.2 = (s32[256]{0:T(256)S(1)}, s32[256]{0:T(256)}, u32[]{:S(2)}) copy-start(s32[256]{0:T(256)} %param.8) | copy-start | bytes 3076
  5.2 138.0 %all-to-all-start = ((bf16[16,1,2,256,512]{4,3,2,1,0:T(8,128)(2,1)}), bf16[16,1,2,256,512]{4,3,2,1,0:T(8,128)(2,1)}, u32[]{:S(2)}, u32[]{:S(2)}) async-start(bf16[16,1,2,256,512]{4,3,2,1,0:T(8,128)(2,1)} %stack.9), calls=%async_computation | async-start | bytes 16777216 | tf_op jit(solution)/shard_map/all_to_all | solution.py:22
  151.4 23.7 %copy-start = (bf16[8,2,256,1]{2,0,1,3:T(8,128)(2,1)S(1)}, bf16[8,2,256,1]{2,0,1,3:T(8,128)(2,1)}, u32[]{:S(2)}) copy-start(bf16[8,2,256,1]{2,0,1,3:T(8,128)(2,1)} %constant.39) | copy-start | bytes 24580
  151.4 24.4 %copy-start.1 = (bf16[8,2,256,1]{2,0,1,3:T(8,128)(2,1)S(1)}, bf16[8,2,256,1]{2,0,1,3:T(8,128)(2,1)}, u32[]{:S(2)}) copy-start(bf16[8,2,256,1]{2,0,1,3:T(8,128)(2,1)} %constant.40) | copy-start | bytes 24580
